TPU v7x, 128 devices: a whole 4x4x4 slice. The times are simulated.
128 devices in a mesh: row: 8 (over y, core), col: 16 (over z, x).
Axes of the slice: x: 4, y: 4, z: 4, core: 2. Of those that a mesh axis runs over, the one named last changes fastest.
Arguments:
- features: float32 [256, 1024, 128], P('row', 'col'), may hold values from -0.4 to 0.4
- step_size: float32 [256, 1024, 128], P('row', 'col'), may hold values from 0.5 to 2
- write_weights: float32 [256, 1024, 16], P('row', 'col'), may hold values from -6 to 6
- read_weights: float32 [256, 1024, 16], P('row', 'col'), may hold values from -6 to 6
- decay_log: float32 [16, 128], replicated, may hold values from -7.6 to -3.5
- out_grad: float32 [256, 1024, 128], P('row', 'col'), may hold values from -0.4 to 0.4
Outputs:
- grad_features: float32 [256, 1024, 128], P('row', 'col')
- grad_step: float32 [256, 1024, 128], P('row', 'col')
- grad_write: float32 [256, 1024, 16], P('row', 'col')
- grad_read: float32 [256, 1024, 16], P('row', 'col')
- grad_decay: float32 [16, 128], replicated
All inputs are finite; a program needn't handle non-finite values.
Results may differ from a plain program's by a relative error of at most 0.0002.
Values sent between devices are 32-bit elements; how exact they have to be, the bound alone decides.
A program may use at most 320 MiB of HBM per device.

v0:
```python
import jax
import jax.numpy as jnp
from jax import lax
from jax.sharding import PartitionSpec as P


def carried_in(shard, axis, combine, identity, reverse):
    size, mine = (lax.axis_size(axis), lax.axis_index(axis))
    everything = jax.tree.map(lambda part: lax.all_gather(part, axis), shard)
    start = jax.tree.map(
        lambda part, zero: jnp.broadcast_to(jnp.asarray(zero, part.dtype), part.shape),
        shard,
        identity,
    )

    def lap(k, before):
        at = size - 1 - k if reverse else k
        reached = at > mine if reverse else at < mine
        new = combine(before, jax.tree.map(lambda part: part[at], everything))
        return jax.tree.map(lambda a, b: jnp.where(reached, a, b), new, before)

    return lax.fori_loop(0, size, lap, start)


def sweep_rows(decays, driving, backward):

    def advance(current, inputs):
        factor, source = inputs
        current = factor * current + source
        return (current, current)

    def retreat(passed, inputs):
        factor, source = inputs
        adjoint = source + passed
        return (factor * adjoint, adjoint)

    initial = jnp.zeros(decays.shape[1:], jnp.float32)
    if backward:
        closing, values = lax.scan(retreat, initial, (decays, driving), reverse=True)
    else:
        closing, values = lax.scan(advance, initial, (decays, driving))
    return (values, closing)


def sweep_cols(decays, driving, backward):
    length = decays.shape[1]

    def advance(index, running):
        current, values = running
        place = length - 1 - index if backward else index
        place = jnp.asarray(place).astype(jnp.int32)
        factor = lax.dynamic_index_in_dim(decays, place, 1, keepdims=False)
        source = lax.dynamic_index_in_dim(driving, place, 1, keepdims=False)
        if backward:
            value = source + current
            values = lax.dynamic_update_index_in_dim(values, value, place, 1)
            current = factor * value
        else:
            current = factor * current + source
            values = lax.dynamic_update_index_in_dim(values, current, place, 1)
        return (current, values)

    initial = jnp.zeros(decays.shape[:1] + decays.shape[2:], jnp.float32)
    closing, values = lax.fori_loop(0, length, advance, (initial, jnp.zeros_like(driving)))
    return (values, closing)


def link_parts(final_state, exponent_sum, decay_rate):

    def combine(earlier, subsequent):
        return (earlier[0] * subsequent[0], subsequent[0] * earlier[1] + subsequent[1])

    products = jnp.exp(exponent_sum[:, None, :] * decay_rate)
    element = (products, final_state)
    identity = (jnp.ones_like(products), jnp.zeros_like(final_state))
    return (element, identity, combine)


def shards(features, step_size, write_weights, read_weights, decay_log, out_grad):
    highest = lax.Precision.HIGHEST
    decay_rate = -jnp.exp(decay_log)
    decays = jnp.exp(step_size[:, :, None, :] * decay_rate)
    driving = step_size[:, :, None, :] * write_weights[:, :, :, None] * features[:, :, None, :]
    running_rows = jnp.cumsum(step_size, 0)
    running_cols = jnp.cumsum(step_size, 1)
    sum_rows = running_rows[-1]
    sum_cols = running_cols[:, -1]
    local_rows, leaving_rows = sweep_rows(decays, driving, False)
    element, identity, combine = link_parts(leaving_rows, sum_rows, decay_rate)
    from_above = carried_in(element, "row", combine, identity, False)[1]
    vertical = local_rows + jnp.exp(running_rows[:, :, None, :] * decay_rate) * from_above[None]
    vert_prev = jnp.concatenate([from_above[None], vertical[:-1]], 0)
    local_cols, leaving_cols = sweep_cols(decays, vertical, False)
    element, identity, combine = link_parts(leaving_cols, sum_cols, decay_rate)
    from_left = carried_in(element, "col", combine, identity, False)[1]
    states = local_cols + jnp.exp(running_cols[:, :, None, :] * decay_rate) * from_left[:, None]
    states_prev = jnp.concatenate([from_left[:, None], states[:, :-1]], 1)
    direct = read_weights[:, :, :, None] * out_grad[:, :, None, :]
    adjoint_local, outgoing_cols = sweep_cols(decays, direct, True)
    element, identity, combine = link_parts(outgoing_cols, sum_cols, decay_rate)
    from_right = carried_in(element, "col", combine, identity, True)[1]
    after_cols = sum_cols[:, None, :] - running_cols
    adjoint_h = (
        adjoint_local + jnp.exp(after_cols[:, :, None, :] * decay_rate) * from_right[:, None]
    )
    adjoint_vlocal, outgoing_rows = sweep_rows(decays, adjoint_h, True)
    element, identity, combine = link_parts(outgoing_rows, sum_rows, decay_rate)
    from_below = carried_in(element, "row", combine, identity, True)[1]
    after_rows = sum_rows[None] - running_rows
    adjoint_v = adjoint_vlocal + jnp.exp(after_rows[:, :, None, :] * decay_rate) * from_below[None]
    exponent_grad = (adjoint_h * states_prev + adjoint_v * vert_prev) * decays
    through = jnp.einsum("hwnd,hwn->hwd", adjoint_v, write_weights, precision=highest)
    grad_features = step_size * through
    grad_step = features * through + jnp.einsum(
        "hwnd,nd->hwd", exponent_grad, decay_rate, precision=highest
    )
    grad_write = jnp.einsum("hwnd,hwd->hwn", adjoint_v, step_size * features, precision=highest)
    grad_read = jnp.einsum("hwnd,hwd->hwn", states, out_grad, precision=highest)
    partial_sum = jnp.einsum("hwnd,hwd->nd", exponent_grad, step_size, precision=highest)
    grad_decay = lax.psum(partial_sum, ("row", "col")) * decay_rate
    return (grad_features, grad_step, grad_write, grad_read, grad_decay)


def solution(mesh):
    in_specs = (
        P("row", "col", None),
        P("row", "col", None),
        P("row", "col", None),
        P("row", "col", None),
        P(),
        P("row", "col", None),
    )
    out_specs = (
        P("row", "col", None),
        P("row", "col", None),
        P("row", "col", None),
        P("row", "col", None),
        P(),
    )
    return jax.shard_map(shards, mesh=mesh, in_specs=in_specs, out_specs=out_specs, check_vma=False)
```

profile of v0, /device:TPU:1, one launch (start us, length us, event | category | flops | bytes accessed | tf_op | source)
XLA Modules:
  0.0 968.1 jit_solution(15481916507911445551)
XLA Ops:
  13.7 9.3 multiply_multiply_fusion
  23.0 5.8 copy-done
  28.8 6.2 copy.32
  35.0 7.9 broadcast.59.clone3
  42.9 79.4 %while.128 = (s32[]{:T(128)}, f32[64,16,128]{2,1,0:T(8,128)S(1)}, f32[32,64,16,128]{3,2,0,1:T(8,128)}, f32[32,64,16,128]{3,2,1,0:T(8,128)}, f32[32,64,16,128]{3,2,0,1:T(8,128)}, /*index=5*/s32[]{:T(128)}, s32[]{:T(128)}) while((s32[]{:T(128)}, f32[64,16,128]{2,1,0:T(8,128)S(1)}, f32[32,64,16,128]{3,2,0,1:T(8,128)}, ...), condition=%wide.region_11.12_spmd.clone, body=%wide.region_10.11_spmd.clone.sunk | while | flops 393219 | bytes 2622039 | solution.py:41
  42.9 2.5 bitcast_dynamic-update-slice_fusion.10
  45.4 2.5 bitcast_dynamic-update-slice_fusion.10
  47.9 2.5 bitcast_dynamic-update-slice_fusion.10
  50.4 2.5 bitcast_dynamic-update-slice_fusion.10
  52.9 2.5 bitcast_dynamic-update-slice_fusion.10
  57.9 2.5 bitcast_dynamic-update-slice_fusion.10
  60.4 2.5 bitcast_dynamic-update-slice_fusion.10
  62.8 2.5 bitcast_dynamic-update-slice_fusion.10
  65.3 2.5 bitcast_dynamic-update-slice_fusion.10
  67.8 2.5 bitcast_dynamic-update-slice_fusion.10
  70.3 2.5 bitcast_dynamic-update-slice_fusion.10
  82.6 2.5 bitcast_dynamic-update-slice_fusion.10
  90.1 2.5 bitcast_dynamic-update-slice_fusion.10
  95.0 2.5 bitcast_dynamic-update-slice_fusion.10
  97.5 2.5 bitcast_dynamic-update-slice_fusion.10
  109.9 2.5 bitcast_dynamic-update-slice_fusion.10
  119.8 2.5 bitcast_dynamic-update-slice_fusion.10
  123.2 4.0 fusion.18
  134.2 7.6 broadcast_multiply_fusion
  141.8 8.0 broadcast.59.clone3.2
  149.7 186.2 %while.124 = (s32[]{:T(128)}, f32[32,16,128]{2,1,0:T(8,128)S(1)}, f32[32,64,16,128]{3,2,0,1:T(8,128)}, f32[32,64,16,128]{3,2,0,1:T(8,128)}, f32[32,64,16,128]{3,...) while((s32[]{:T(128)}, f32[32,16,128]{2,1,0:T(8,128)S(1)}, ...), condition=%wide.region_1.2_spmd.clone, body=%wide.region_0.0_spmd.clone.sunk | while | flops 327687 | bytes 1835166 | solution.py:64
  338.5 13.5 %while.129 = (s32[]{:T(128)}, f32[64,16,128]{2,1,0:T(8,128)S(1)}, s32[]{:T(128)}, f32[8,64,16,128]{3,2,1,0:T(8,128)}, f32[8,64,16,128]{3,2,1,0:T(8,128)}, /*index=5*/s32[]{:T(128)}, s32[]{:T(128)}) while((s32[]{:T(128)}, f32[64,16,128]{2,1,0:T(8,128)S(1)}, s32[]{:T(128)}, f32[8,64,16,128]{3,2,1,0:T(8,128)}, ...), condition=%wide.region_13.14_spmd.clone, body=%wide.region_12.13_spmd.clone.sunk | while | flops 524292 | bytes 2097253 | solution.py:22
  352.0 12.2 %multiply_add_fusion.1 = f32[32,64,16,128]{3,2,0,1:T(8,128)} fusion(f32[32,64,16,128]{3,2,0,1:T(8,128)} %get-tuple-element.823, f32[64,16,128]{2,1,0:T(8,128)S(1)} %get-tuple-element.825, f32[32,64,128]{2,0,1:T(8,128)} %copy.41, f32[16,128]{1,0:T(8,128)S(1)} %exponential_negate_fusion), kind=kLoop, calls=%fused_computation.33 | loop fusion | flops 12582912 | bytes 35135488 | tf_op jit(solution)/shard_map/add | solution.py:91
  364.2 8.0 broadcast.59.clone3.1
  372.2 124.9 %while.130 = (s32[]{:T(128)}, f32[32,16,128]{2,1,0:T(8,128)S(1)}, f32[32,64,16,128]{3,2,0,1:T(8,128)}, f32[32,64,16,128]{3,2,0,1:T(8,128)}, f32[32,64,16,128]{3,2,0,1:T(8,128)}, /*index=5*/s32[]{:T(128)}, s32[]{:T(128)}) while((s32[]{:T(128)}, f32[32,16,128]{2,1,0:T(8,128)S(1)}, f32[32,64,16,128]{3,2,0,1:T(8,128)}, ...), condition=%wide.region_15.16_spmd.clone, body=%wide.region_14.15_spmd.clone.sunk | while | flops 196611 | bytes 1311319 | solution.py:64
  500.2 29.8 %while.125 = (s32[]{:T(128)}, f32[32,16,128]{2,1,0:T(8,128)}, s32[]{:T(128)}, f32[16,32,16,128]{3,2,1,0:T(8,128)}, f32[16,32,16,128]{3,2,1,0:T(8,128)}, /*index=5*/s32[]{:T(128)}, s32[]{:T(128)}, s32[]{:T(128)}, s32[]{:T(128)}) while((s32[]{:T(128)}, f32[32,16,128]{2,1,0:T(8,128)}, s32[]{:T(128)}, f32[16,32,16,128]{3,2,1,0:T(8,128)}, ...), condition=%wide.region_4.5_spmd.clone, body=%wide.region_3.4_spmd.clone.sunk | while | flops 262152 | bytes 1048739 | solution.py:22
  530.0 22.9 %all-gather.21.cloned.1.call-done = f32[512,16,128]{2,1,0:T(8,128)} async-done(((f32[32,16,128]{2,1,0:T(8,128)}), f32[512,16,128]{2,1,0:T(8,128)}) %all-gather.21.cloned.1.call-update) | async-done | bytes 4194320 | tf_op jit(solution)/shard_map/all_gather | solution.py:9
  552.9 20.3 %while.131 = (s32[]{:T(128)}, f32[32,16,128]{2,1,0:T(8,128)S(1)}, s32[]{:T(128)}, f32[16,32,16,128]{3,2,1,0:T(8,128)}, f32[16,32,16,128]{3,2,1,0:T(8,128)}, /*index=5*/s32[]{:T(128)}, s32[]{:T(128)}) while((s32[]{:T(128)}, f32[32,16,128]{2,1,0:T(8,128)S(1)}, s32[]{:T(128)}, f32[16,32,16,128]{3,2,1,0:T(8,128)}, ...), condition=%wide.region_17.18_spmd.clone, body=%wide.region_16.17_spmd.clone.sunk | while | flops 262148 | bytes 1048677 | solution.py:22
  573.2 23.2 %multiply_add_fusion = (f32[32,64,16,128]{3,2,0,1:T(8,128)}, f32[32,64,16,128]{3,2,0,1:T(8,128)}) fusion(f32[32,64,16,128]{3,2,0,1:T(8,128)} %get-tuple-element.828, f32[32,16,128]{2,1,0:T(8,128)S(1)} %get-tuple-element.827, f32[32,64,128]{2,0,1:T(8,128)} %copy-done.5, f32[16,128]{1,0:T(8,128)S(1)} %exponential_negate_fusion, ...), kind=kLoop, calls=%fused_computation.32 | loop fusion | flops 25165824 | bytes 69738496 | tf_op jit(solution)/shard_map/add | solution.py:96
  596.4 7.9 broadcast.59.clone2
  604.3 113.4 %while.126 = (s32[]{:T(128)}, f32[64,16,128]{2,1,0:T(8,128)S(1)}, f32[32,64,16,128]{3,2,0,1:T(8,128)}, f32[32,64,16,128]{3,2,1,0:T(8,128)}, f32[32,64,16,128]{3,...) while((s32[]{:T(128)}, f32[64,16,128]{2,1,0:T(8,128)S(1)}, f32[32,64,16,128]{3,2,0,1:T(8,128)}, ...), condition=%wide.region_6.7_spmd.clone, body=%wide.region_5.6_spmd.clone.sunk | while | flops 655364 | bytes 3670132 | solution.py:39
  721.8 2.9 copy.44
  724.7 11.6 %slice.19 = f32[31,64,16,128]{3,2,0,1:T(8,128)} slice(f32[32,64,16,128]{3,2,0,1:T(8,128)} %get-tuple-element.1542), slice={[0:31], [0:64], [0:16], [0:128]} | slice | bytes 32505856 | tf_op jit(solution)/shard_map/slice | solution.py:92
  736.3 13.9 %slice.18 = f32[32,63,16,128]{3,2,0,1:T(8,128)} slice(f32[32,64,16,128]{3,2,0,1:T(8,128)} %get-tuple-element.1087), slice={[0:32], [0:63], [0:16], [0:128]} | slice | bytes 33030144 | tf_op jit(solution)/shard_map/slice | solution.py:97
  753.5 27.6 %fusion.6 = f32[32,64,1,16]{3,2,1,0:T(1,128)} fusion(f32[32,64,128,1]{2,3,1,0:T(1,128)S(1)} %bitcast.158, f32[32,64,16,128]{3,2,0,1:T(8,128)S(1)} %bitcast.152), kind=kOutput, calls=%fused_computation.29 | convolution fusion | flops 50331648 | bytes 17956864 | tf_op jit(solution)/shard_map/hwnd,hwd->hwn/dot_general | solution.py:118
  781.1 2.9 copy.57
  784.1 13.5 %while.127 = (s32[]{:T(128)}, f32[64,16,128]{2,1,0:T(8,128)S(1)}, s32[]{:T(128)}, f32[8,64,16,128]{3,2,1,0:T(8,128)}, f32[8,64,16,128]{3,2,1,0:T(8,128)}, /*index=5*/s32[]{:T(128)}, s32[]{:T(128)}, s32[]{:T(128)}, s32[]{:T(128)}) while((s32[]{:T(128)}, f32[64,16,128]{2,1,0:T(8,128)S(1)}, s32[]{:T(128)}, ...), condition=%wide.region_9.10_spmd.clone, body=%wide.region_8.9_spmd.clone.sunk | while | flops 524296 | bytes 2097315 | solution.py:22
  797.6 34.8 %multiply_reduce_fusion = (f32[128,16]{0,1:T(8,128)S(1)}, f32[32,64,16,128]{3,2,0,1:T(8,128)}, f32[32,64,16,128]{3,2,0,1:T(8,128)}) fusion(f32[128,32,64]{0,1,2:T(8,128)} %copy.74, f32[16,128]{1,0:T(8,128)S(1)} %exponential_negate_fusion, f32[32,64,128]{2,0,1:T(8,128)S(1)} %copy-done.7, f32[31,64,16,128]{3,2,0,1:T(8,128)} %slice.19, ...), kind=kLoop, calls=%fused_computation.28 | loop fusion | flops 50329600 | bytes 104349696 | tf_op jit(solution)/shard_map/hwnd,hwd->nd/dot_general | solution.py:119
  832.3 64.6 %psum.7 = f32[16,128]{1,0:T(8,128)S(1)} all-reduce(f32[16,128]{1,0:T(8,128)S(1)} %bitcast.166), channel_id=1, replica_groups=mesh['row'=8,'col'=16] {'row','col'}, use_global_device_ids=true, to_apply=%region_18.19 | all-reduce | flops 2048 | bytes 16384 | tf_op jit(solution)/shard_map/psum | solution.py:120
  897.5 18.2 %fusion.10 = f32[32,64,1,128]{3,2,1,0:T(1,128)S(1)} fusion(f32[32,64,16,1]{2,3,1,0:T(1,128)} %copy.44, f32[32,64,16,128]{3,2,0,1:T(8,128)} %get-tuple-element.1079), kind=kOutput, calls=%fused_computation.40 | convolution fusion | flops 50331648 | bytes 17956864 | tf_op jit(solution)/shard_map/hwnd,hwn->hwd/dot_general | solution.py:112
  915.7 10.9 %multiply_reduce_fusion.1 = f32[128,32,64]{0,1,2:T(8,128)} fusion(f32[32,64,16,128]{3,2,0,1:T(8,128)} %get-tuple-element.1078, f32[128,16]{0,1:T(8,128)S(1)} %get-tuple-element.1086), kind=kLoop, calls=%fused_computation.31 | loop fusion | flops 8126464 | bytes 17833984
  926.6 3.6 fusion.17
  930.2 28.9 %fusion.8 = f32[32,64,1,16]{3,2,1,0:T(1,128)S(1)} fusion(f32[32,64,128,1]{2,3,1,0:T(1,128)S(1)} %bitcast.157, f32[32,64,16,128]{3,2,0,1:T(8,128)} %get-tuple-element.1079), kind=kOutput, calls=%fused_computation.38 | convolution fusion | flops 50331648 | bytes 17956864 | tf_op jit(solution)/shard_map/hwnd,hwd->hwn/dot_general | solution.py:117
  (394 shorter events, 565.5 us)
Async XLA Ops:
  7.2 331.3 %all-gather.19.cloned.1.call-start = ((), (), s32[]{:S(2)}) async-start(), calls=%async_computation.4 | async-start | bytes 4718592 | tf_op jit(solution)/shard_map/all_gather | solution.py:9
  9.8 13.2 %copy-start.6 = (f32[32,64,128]{2,0,1:T(8,128)}, f32[32,64,128]{2,0,1:T(8,128)S(1)}, u32[]{:S(2)}) copy-start(f32[32,64,128]{2,0,1:T(8,128)S(1)} %copy.27) | copy-start | bytes 3145732
  23.0 5.8 copy-start
  35.0 88.2 %copy-start.3 = (f32[32,64,128]{2,1,0:T(8,128)S(1)}, f32[32,64,128]{2,1,0:T(8,128)}, u32[]{:S(2)}) copy-start(f32[32,64,128]{2,1,0:T(8,128)} %param.23) | copy-start | bytes 3145732
  35.0 95.6 %copy-start.10 = (f32[32,64,16]{1,2,0:T(8,128)S(1)}, f32[32,64,16]{1,2,0:T(8,128)}, u32[]{:S(2)}) copy-start(f32[32,64,16]{1,2,0:T(8,128)} %param.25) | copy-start | bytes 393220
  122.3 0.8 copy-start.4
  123.1 215.4 %all-gather.13.cloned.1.call-start = ((), (), s32[]{:S(2)}) async-start(), calls=%async_computation.1 | async-start | bytes 4718592 | tf_op jit(solution)/shard_map/all_gather | solution.py:9
  128.1 372.1 %all-gather.11.cloned.1.call-start = ((), (), s32[]{:S(2)}) async-start(), calls=%async_computation | async-start | bytes 4456448 | tf_op jit(solution)/shard_map/all_gather | solution.py:9
  128.7 1.0 copy-start.5
  130.5 369.7 %all-gather.15.cloned.1.call-start = ((), (), s32[]{:S(2)}) async-start(), calls=%async_computation.2 | async-start | bytes 4456448 | tf_op jit(solution)/shard_map/all_gather | solution.py:9
  336.0 0.7 copy-start.2
  336.7 216.2 %all-gather.21.cloned.1.call-start = ((), (), s32[]{:S(2)}) async-start(), calls=%async_computation.5 | async-start | bytes 4456448 | tf_op jit(solution)/shard_map/all_gather | solution.py:9
  497.1 0.7 copy-start.8
  497.8 286.3 %all-gather.17.cloned.1.call-start = ((), (), s32[]{:S(2)}) async-start(), calls=%async_computation.3 | async-start | bytes 4718592 | tf_op jit(solution)/shard_map/all_gather | solution.py:9
  717.7 0.8 copy-start.1
  736.2 14.0 %slice-start = ((s8[16777216]{0:T(1024)(128)(4,1)}), s8[4194304]{0:T(1024)(128)(4,1)S(1)}, s32[]{:S(2)}) async-start(s8[16777216]{0:T(1024)(128)(4,1)} %bitcast.151), calls=%async_computation.6 | async-start | bytes 8388608
  736.2 14.0 %copy-start.9 = (f32[32,64,128]{2,1,0:T(8,128)S(1)}, f32[32,64,128]{2,1,0:T(8,128)}, u32[]{:S(2)}) copy-start(f32[32,64,128]{2,1,0:T(8,128)} %param.27) | copy-start | bytes 3145732
  736.2 14.6 %slice-start.1 = ((s8[16777216]{0:T(1024)(128)(4,1)}), s8[4194304]{0:T(1024)(128)(4,1)S(1)}, s32[]{:S(2)}) async-start(s8[16777216]{0:T(1024)(128)(4,1)} %bitcast.151), calls=%async_computation.7 | async-start | bytes 8388608
  736.3 16.1 %slice-start.2 = ((s8[16777216]{0:T(1024)(128)(4,1)}), s8[4194304]{0:T(1024)(128)(4,1)S(1)}, s32[]{:S(2)}) async-start(s8[16777216]{0:T(1024)(128)(4,1)} %bitcast.151), calls=%async_computation.8 | async-start | bytes 8388608
  736.3 17.2 %slice-start.3 = ((s8[16777216]{0:T(1024)(128)(4,1)}), s8[4194304]{0:T(1024)(128)(4,1)S(1)}, s32[]{:S(2)}) async-start(s8[16777216]{0:T(1024)(128)(4,1)} %bitcast.151), calls=%async_computation.9 | async-start | bytes 8388608
  753.5 44.0 %copy-start.7 = (f32[32,64,128]{2,0,1:T(8,128)S(1)}, f32[32,64,128]{2,0,1:T(8,128)}, u32[]{:S(2)}) copy-start(f32[32,64,128]{2,0,1:T(8,128)} %copy-done.6) | copy-start | bytes 3145732
  797.6 99.3 %copy-start.11 = (f32[16,128]{1,0:T(8,128)S(1)}, f32[16,128]{1,0:T(8,128)}, u32[]{:S(2)}) copy-start(f32[16,128]{1,0:T(8,128)} %param.26) | copy-start | bytes 24580
Sparse Core Ops, SparseCore 0:
  123.2 35.7 all-gather.18
  160.7 32.0 all-gather.12
  195.6 51.1 all-gather.10
  336.8 54.8 all-gather.14
  497.9 54.8 all-gather.20
  718.6 32.1 all-gather.16
where the time goes:
time: 984 us; the launch traced here: 968 us
  other arithmetic  690 us (70%)
  local copies, waits for them, and re-layouts  98.4 us (10%)
  matrix products  74.7 us (8%)
  blocking collectives  64.6 us (7%)
  waiting for transfers between devices  23 us (2%)
  between operations  14.6 us (1%)
    dynamic_update_slice x64, other arithmetic, sweep_rows(): closing, values = lax.scan(advance, initial, (decays, driving))  143 us
    dynamic_update_slice x64, other arithmetic, advance(): values = lax.dynamic_update_index_in_dim(values, current, place, 1)  125 us
    dynamic_update_slice x64, other arithmetic, advance(): values = lax.dynamic_update_index_in_dim(values, value, place, 1)  108 us
    mul x64, other arithmetic, advance(): current = factor * value  76.4 us
    select_n x48, other arithmetic, lap(): return jax.tree.map(lambda a, b: jnp.where(reached, a, b), new, before)  76.4 us
    psum x1, blocking collectives, shards(): grad_decay = lax.psum(partial_sum, ('row', 'col')) * decay_rate  64.6 us
    mul x32, other arithmetic, retreat(): return (factor * adjoint, adjoint)  49.2 us
    dot_general x1, other arithmetic, shards(): jnp.einsum('hwnd,hwd->nd', exponent_grad, step_size, precision=highest)  34.8 us
  transfers between devices with their start and end apart: 6, of which 1 were waited for; matrix products, arithmetic and copies ran while one was open for 48% of the time, Pallas kernels for 0%

commit v1 on v0

--- a/solution.py
+++ b/solution.py
@@ -117,7 +117,7 @@
     grad_write = jnp.einsum("hwnd,hwd->hwn", adjoint_v, step_size * features, precision=highest)
     grad_read = jnp.einsum("hwnd,hwd->hwn", states, out_grad, precision=highest)
     partial_sum = jnp.einsum("hwnd,hwd->nd", exponent_grad, step_size, precision=highest)
-    grad_decay = lax.psum(partial_sum, ("row", "col")) * decay_rate
+    grad_decay = jnp.sum(lax.all_gather(partial_sum, ("row", "col")), axis=0) * decay_rate
     return (grad_features, grad_step, grad_write, grad_read, grad_decay)
 
 

time: 984 us -> 933 us (0.948)
  blocking collectives: 64.6 us -> 0 us
  waiting for transfers between devices: 23 us -> 41.7 us
    psum x1 -> x0, blocking collectives: 64.6 us -> none  [shards(): grad_decay = lax.psum(partial_sum, ('row', 'col')) * decay_rate]
    all_gather x0 -> x1, waiting for transfers between devices: none -> 11.6 us  [shards(): lax.all_gather(partial_sum, ('row', 'col'))]
    unnamed x40 -> x38, local copies, waits for them, and re-layouts: 33.1 us -> 32.1 us
  transfers between devices with their start and end apart: 6 -> 7, of which waited for: 1 -> 3; matrix products, arithmetic and copies ran while one was open for 48% -> 52% of each run, Pallas kernels for 0% -> 0%
where the time goes in v1:
time: 933 us; the launch traced here: 917 us
  other arithmetic  691 us (74%)
  local copies, waits for them, and re-layouts  90.2 us (10%)
  matrix products  76.1 us (8%)
  waiting for transfers between devices  41.7 us (4%)
  between operations  14.8 us (2%)
    dynamic_update_slice x64, other arithmetic, sweep_rows(): closing, values = lax.scan(advance, initial, (decays, driving))  141 us
    dynamic_update_slice x64, other arithmetic, advance(): values = lax.dynamic_update_index_in_dim(values, current, place, 1)  125 us
    dynamic_update_slice x64, other arithmetic, advance(): values = lax.dynamic_update_index_in_dim(values, value, place, 1)  109 us
    select_n x48, other arithmetic, lap(): return jax.tree.map(lambda a, b: jnp.where(reached, a, b), new, before)  76.4 us
    mul x64, other arithmetic, advance(): current = factor * value  76.3 us
    mul x32, other arithmetic, retreat(): return (factor * adjoint, adjoint)  49.2 us
    dot_general x1, other arithmetic, shards(): jnp.einsum('hwnd,hwd->nd', exponent_grad, step_size, precision=highest)  35.4 us
    unnamed x38, local copies, waits for them, and re-layouts  32.1 us
  transfers between devices with their start and end apart: 7, of which 3 were waited for; matrix products, arithmetic and copies ran while one was open for 52% of the time, Pallas kernels for 0%

profile of v1, /device:TPU:1, one launch (start us, length us, event | category | flops | bytes accessed | tf_op | source)
XLA Modules:
  0.0 917.2 jit_solution(5525591677716512331)
XLA Ops:
  13.7 9.3 %multiply_multiply_fusion = (f32[32,64,16,128]{3,2,0,1:T(8,128)}, f32[32,64,16,128]{3,2,0,1:T(8,128)S(1)}) fusion(f32[32,64,128]{2,0,1:T(8,128)S(1)} %copy.53, f32[32,64,16]{2,0,1:T(8,128)S(1)} %copy.52, f32[32,64,128]{2,0,1:T(8,128)S(1)} %copy.43, f32[16,128]{1,0:T(8,128)S(1)} %exponential_negate_fusion), kind=kLoop, calls=%fused_computation.34 | loop fusion | flops 12582912 | bytes 35790848 | tf_op jit(solution)/shard_map/mul | solution.py:83
  23.0 5.7 copy-done
  28.8 6.2 copy.48
  34.9 7.8 broadcast.59.clone3
  42.7 79.3 %while.128 = (s32[]{:T(128)}, f32[64,16,128]{2,1,0:T(8,128)S(1)}, f32[32,64,16,128]{3,2,0,1:T(8,128)}, f32[32,64,16,128]{3,2,1,0:T(8,128)}, f32[32,64,16,128]{3,2,0,1:T(8,128)}, /*index=5*/s32[]{:T(128)}, s32[]{:T(128)}) while((s32[]{:T(128)}, f32[64,16,128]{2,1,0:T(8,128)S(1)}, f32[32,64,16,128]{3,2,0,1:T(8,128)}, ...), condition=%wide.region_11.12_spmd.clone, body=%wide.region_10.11_spmd.clone.sunk | while | flops 393219 | bytes 2622039 | solution.py:41
  42.7 2.5 bitcast_dynamic-update-slice_fusion.10
  45.3 2.5 bitcast_dynamic-update-slice_fusion.10
  50.2 2.5 bitcast_dynamic-update-slice_fusion.10
  52.7 2.5 bitcast_dynamic-update-slice_fusion.10
  55.2 2.5 bitcast_dynamic-update-slice_fusion.10
  57.7 2.5 bitcast_dynamic-update-slice_fusion.10
  67.6 2.5 bitcast_dynamic-update-slice_fusion.10
  72.5 2.5 bitcast_dynamic-update-slice_fusion.10
  77.5 2.5 bitcast_dynamic-update-slice_fusion.10
  80.0 2.5 bitcast_dynamic-update-slice_fusion.10
  82.5 2.5 bitcast_dynamic-update-slice_fusion.10
  85.0 2.5 bitcast_dynamic-update-slice_fusion.10
  87.5 2.5 bitcast_dynamic-update-slice_fusion.10
  92.4 2.5 bitcast_dynamic-update-slice_fusion.10
  112.1 2.5 bitcast_dynamic-update-slice_fusion.10
  117.0 2.5 bitcast_dynamic-update-slice_fusion.10
  119.5 2.5 bitcast_dynamic-update-slice_fusion.10
  122.9 4.0 fusion.18
  133.9 7.5 broadcast_multiply_fusion
  141.4 8.0 broadcast.59.clone3.2
  149.4 186.5 %while.124 = (s32[]{:T(128)}, f32[32,16,128]{2,1,0:T(8,128)S(1)}, f32[32,64,16,128]{3,2,0,1:T(8,128)}, f32[32,64,16,128]{3,2,0,1:T(8,128)}, f32[32,64,16,128]{3,...) while((s32[]{:T(128)}, f32[32,16,128]{2,1,0:T(8,128)S(1)}, ...), condition=%wide.region_1.2_spmd.clone, body=%wide.region_0.0_spmd.clone.sunk | while | flops 327687 | bytes 1835166 | solution.py:64
  338.8 13.5 %while.129 = (s32[]{:T(128)}, f32[64,16,128]{2,1,0:T(8,128)S(1)}, s32[]{:T(128)}, f32[8,64,16,128]{3,2,1,0:T(8,128)}, f32[8,64,16,128]{3,2,1,0:T(8,128)}, /*index=5*/s32[]{:T(128)}, s32[]{:T(128)}) while((s32[]{:T(128)}, f32[64,16,128]{2,1,0:T(8,128)S(1)}, s32[]{:T(128)}, f32[8,64,16,128]{3,2,1,0:T(8,128)}, ...), condition=%wide.region_13.14_spmd.clone, body=%wide.region_12.13_spmd.clone.sunk | while | flops 524292 | bytes 2097253 | solution.py:22
  352.3 12.2 %multiply_add_fusion.1 = f32[32,64,16,128]{3,2,0,1:T(8,128)} fusion(f32[32,64,16,128]{3,2,0,1:T(8,128)} %get-tuple-element.823, f32[64,16,128]{2,1,0:T(8,128)S(1)} %get-tuple-element.825, f32[32,64,128]{2,0,1:T(8,128)} %copy.57, f32[16,128]{1,0:T(8,128)S(1)} %exponential_negate_fusion), kind=kLoop, calls=%fused_computation.33 | loop fusion | flops 12582912 | bytes 35135488 | tf_op jit(solution)/shard_map/add | solution.py:91
  364.5 8.0 broadcast.59.clone3.1
  372.5 125.3 %while.130 = (s32[]{:T(128)}, f32[32,16,128]{2,1,0:T(8,128)S(1)}, f32[32,64,16,128]{3,2,0,1:T(8,128)}, f32[32,64,16,128]{3,2,0,1:T(8,128)}, f32[32,64,16,128]{3,2,0,1:T(8,128)}, /*index=5*/s32[]{:T(128)}, s32[]{:T(128)}) while((s32[]{:T(128)}, f32[32,16,128]{2,1,0:T(8,128)S(1)}, f32[32,64,16,128]{3,2,0,1:T(8,128)}, ...), condition=%wide.region_15.16_spmd.clone, body=%wide.region_14.15_spmd.clone.sunk | while | flops 196611 | bytes 1311319 | solution.py:64
  500.9 29.8 %while.125 = (s32[]{:T(128)}, f32[32,16,128]{2,1,0:T(8,128)}, s32[]{:T(128)}, f32[16,32,16,128]{3,2,1,0:T(8,128)}, f32[16,32,16,128]{3,2,1,0:T(8,128)}, /*index=5*/s32[]{:T(128)}, s32[]{:T(128)}, s32[]{:T(128)}, s32[]{:T(128)}) while((s32[]{:T(128)}, f32[32,16,128]{2,1,0:T(8,128)}, s32[]{:T(128)}, f32[16,32,16,128]{3,2,1,0:T(8,128)}, ...), condition=%wide.region_4.5_spmd.clone, body=%wide.region_3.4_spmd.clone.sunk | while | flops 262152 | bytes 1048739 | solution.py:22
  530.6 22.9 %all-gather.23.cloned.1.call-done = f32[512,16,128]{2,1,0:T(8,128)} async-done(((f32[32,16,128]{2,1,0:T(8,128)}), f32[512,16,128]{2,1,0:T(8,128)}) %all-gather.23.cloned.1.call-update) | async-done | bytes 4194320 | tf_op jit(solution)/shard_map/all_gather | solution.py:9
  553.6 20.3 %while.131 = (s32[]{:T(128)}, f32[32,16,128]{2,1,0:T(8,128)S(1)}, s32[]{:T(128)}, f32[16,32,16,128]{3,2,1,0:T(8,128)}, f32[16,32,16,128]{3,2,1,0:T(8,128)}, /*index=5*/s32[]{:T(128)}, s32[]{:T(128)}) while((s32[]{:T(128)}, f32[32,16,128]{2,1,0:T(8,128)S(1)}, s32[]{:T(128)}, f32[16,32,16,128]{3,2,1,0:T(8,128)}, ...), condition=%wide.region_17.18_spmd.clone, body=%wide.region_16.17_spmd.clone.sunk | while | flops 262148 | bytes 1048677 | solution.py:22
  573.9 23.1 %multiply_add_fusion = (f32[32,64,16,128]{3,2,0,1:T(8,128)}, f32[32,64,16,128]{3,2,0,1:T(8,128)}) fusion(f32[32,64,16,128]{3,2,0,1:T(8,128)} %get-tuple-element.828, f32[32,16,128]{2,1,0:T(8,128)S(1)} %get-tuple-element.827, f32[32,64,128]{2,0,1:T(8,128)} %copy-done.5, f32[16,128]{1,0:T(8,128)S(1)} %exponential_negate_fusion, ...), kind=kLoop, calls=%fused_computation.32 | loop fusion | flops 25165824 | bytes 69738496 | tf_op jit(solution)/shard_map/add | solution.py:96
  597.0 7.9 broadcast.59.clone2
  604.9 111.9 %while.126 = (s32[]{:T(128)}, f32[64,16,128]{2,1,0:T(8,128)S(1)}, f32[32,64,16,128]{3,2,0,1:T(8,128)}, f32[32,64,16,128]{3,2,1,0:T(8,128)}, f32[32,64,16,128]{3,...) while((s32[]{:T(128)}, f32[64,16,128]{2,1,0:T(8,128)S(1)}, f32[32,64,16,128]{3,2,0,1:T(8,128)}, ...), condition=%wide.region_6.7_spmd.clone, body=%wide.region_5.6_spmd.clone.sunk | while | flops 655364 | bytes 3670132 | solution.py:39
  721.2 13.4 %slice.19 = f32[31,64,16,128]{3,2,0,1:T(8,128)} slice(f32[32,64,16,128]{3,2,0,1:T(8,128)} %get-tuple-element.1553), slice={[0:31], [0:64], [0:16], [0:128]} | slice | bytes 32505856 | tf_op jit(solution)/shard_map/slice | solution.py:92
  736.9 6.1 slice.18
  743.0 7.0 all-gather.19.cloned.1.call-done
  750.0 13.5 %while.127 = (s32[]{:T(128)}, f32[64,16,128]{2,1,0:T(8,128)S(1)}, s32[]{:T(128)}, f32[8,64,16,128]{3,2,1,0:T(8,128)}, f32[8,64,16,128]{3,2,1,0:T(8,128)}, /*index=5*/s32[]{:T(128)}, s32[]{:T(128)}, s32[]{:T(128)}, s32[]{:T(128)}) while((s32[]{:T(128)}, f32[64,16,128]{2,1,0:T(8,128)S(1)}, s32[]{:T(128)}, ...), condition=%wide.region_9.10_spmd.clone, body=%wide.region_8.9_spmd.clone.sunk | while | flops 524296 | bytes 2097315 | solution.py:22
  763.5 35.4 %multiply_reduce_fusion = (f32[128,16]{0,1:T(8,128)}, f32[32,64,16,128]{3,2,0,1:T(8,128)}, f32[32,64,16,128]{3,2,0,1:T(8,128)}) fusion(f32[128,32,64]{0,1,2:T(8,128)} %copy.91, f32[16,128]{1,0:T(8,128)S(1)} %exponential_negate_fusion, f32[32,64,128]{2,0,1:T(8,128)S(1)} %copy-done.7, f32[31,64,16,128]{3,2,0,1:T(8,128)} %slice.19, ...), kind=kLoop, calls=%fused_computation.28 | loop fusion | flops 50329600 | bytes 104349696 | tf_op jit(solution)/shard_map/hwnd,hwd->nd/dot_general | solution.py:119
  798.9 2.9 copy.60
  801.8 28.7 %fusion.6 = f32[32,64,1,16]{3,2,1,0:T(1,128)S(1)} fusion(f32[32,64,128,1]{2,3,1,0:T(1,128)} %bitcast.159, f32[32,64,16,128]{3,2,0,1:T(8,128)} %get-tuple-element.1097), kind=kOutput, calls=%fused_computation.29 | convolution fusion | flops 50331648 | bytes 17956864 | tf_op jit(solution)/shard_map/hwnd,hwd->hwn/dot_general | solution.py:118
  832.5 18.4 %fusion.10 = f32[32,64,1,128]{3,2,1,0:T(1,128)S(1)} fusion(f32[32,64,16,1]{2,3,1,0:T(1,128)} %copy.60, f32[32,64,16,128]{3,2,0,1:T(8,128)} %get-tuple-element.1089), kind=kOutput, calls=%fused_computation.40 | convolution fusion | flops 50331648 | bytes 17956864 | tf_op jit(solution)/shard_map/hwnd,hwn->hwd/dot_general | solution.py:112
  850.9 11.6 %all-gather.25.cloned.1.call-done = f32[2048,128]{1,0:T(8,128)} async-done(((f32[16,128]{1,0:T(8,128)}), f32[2048,128]{1,0:T(8,128)}) %all-gather.25.cloned.1.call-update) | async-done | bytes 1048592 | tf_op jit(solution)/shard_map/all_gather | solution.py:120
  864.5 10.9 %multiply_reduce_fusion.1 = f32[128,32,64]{0,1,2:T(8,128)} fusion(f32[32,64,16,128]{3,2,0,1:T(8,128)} %get-tuple-element.1088, f32[128,16]{0,1:T(8,128)S(1)} %get-tuple-element.1096), kind=kLoop, calls=%fused_computation.31 | loop fusion | flops 8126464 | bytes 17833984
  875.4 3.6 fusion.17
  879.1 28.9 %fusion.8 = f32[32,64,1,16]{3,2,1,0:T(1,128)S(1)} fusion(f32[32,64,128,1]{2,3,1,0:T(1,128)S(1)} %bitcast.158, f32[32,64,16,128]{3,2,0,1:T(8,128)} %get-tuple-element.1089), kind=kOutput, calls=%fused_computation.38 | convolution fusion | flops 50331648 | bytes 17956864 | tf_op jit(solution)/shard_map/hwnd,hwd->hwn/dot_general | solution.py:117
  (395 shorter events, 567.4 us)
Async XLA Ops:
  7.2 331.6 %all-gather.21.cloned.1.call-start = ((), (), s32[]{:S(2)}) async-start(), calls=%async_computation.4 | async-start | bytes 4718592 | tf_op jit(solution)/shard_map/all_gather | solution.py:9
  9.8 13.3 %copy-start.6 = (f32[32,64,128]{2,0,1:T(8,128)}, f32[32,64,128]{2,0,1:T(8,128)S(1)}, u32[]{:S(2)}) copy-start(f32[32,64,128]{2,0,1:T(8,128)S(1)} %copy.43) | copy-start | bytes 3145732
  23.0 5.7 copy-start
  34.9 88.0 %copy-start.3 = (f32[32,64,128]{2,1,0:T(8,128)S(1)}, f32[32,64,128]{2,1,0:T(8,128)}, u32[]{:S(2)}) copy-start(f32[32,64,128]{2,1,0:T(8,128)} %param.23) | copy-start | bytes 3145732
  34.9 95.4 %copy-start.9 = (f32[32,64,16]{1,2,0:T(8,128)S(1)}, f32[32,64,16]{1,2,0:T(8,128)}, u32[]{:S(2)}) copy-start(f32[32,64,16]{1,2,0:T(8,128)} %param.25) | copy-start | bytes 393220
  122.0 0.8 copy-start.4
  122.9 215.9 %all-gather.15.cloned.1.call-start = ((), (), s32[]{:S(2)}) async-start(), calls=%async_computation.1 | async-start | bytes 4718592 | tf_op jit(solution)/shard_map/all_gather | solution.py:9
  127.8 373.0 %all-gather.13.cloned.1.call-start = ((), (), s32[]{:S(2)}) async-start(), calls=%async_computation | async-start | bytes 4456448 | tf_op jit(solution)/shard_map/all_gather | solution.py:9
  128.5 1.0 copy-start.5
  130.3 370.6 %all-gather.17.cloned.1.call-start = ((), (), s32[]{:S(2)}) async-start(), calls=%async_computation.2 | async-start | bytes 4456448 | tf_op jit(solution)/shard_map/all_gather | solution.py:9
  335.9 0.7 copy-start.2
  336.6 216.9 %all-gather.23.cloned.1.call-start = ((), (), s32[]{:S(2)}) async-start(), calls=%async_computation.5 | async-start | bytes 4456448 | tf_op jit(solution)/shard_map/all_gather | solution.py:9
  497.8 0.7 copy-start.8
  498.5 251.5 %all-gather.19.cloned.1.call-start = ((), (), s32[]{:S(2)}) async-start(), calls=%async_computation.3 | async-start | bytes 4718592 | tf_op jit(solution)/shard_map/all_gather | solution.py:9
  716.9 0.8 copy-start.1
  717.7 144.8 %all-gather.25.cloned.1.call-start = ((), (), s32[]{:S(2)}) async-start(), calls=%async_computation.6 | async-start | bytes 1056768 | tf_op jit(solution)/shard_map/all_gather | solution.py:120
  719.6 15.0 %slice-start = ((s8[16777216]{0:T(1024)(128)(4,1)}), s8[4194304]{0:T(1024)(128)(4,1)S(1)}, s32[]{:S(2)}) async-start(s8[16777216]{0:T(1024)(128)(4,1)} %bitcast.152), calls=%async_computation.7 | async-start | bytes 8388608
  721.2 13.4 %slice-start.1 = ((s8[16777216]{0:T(1024)(128)(4,1)}), s8[4194304]{0:T(1024)(128)(4,1)S(1)}, s32[]{:S(2)}) async-start(s8[16777216]{0:T(1024)(128)(4,1)} %bitcast.152), calls=%async_computation.8 | async-start | bytes 8388608
  721.2 14.1 %slice-start.2 = ((s8[16777216]{0:T(1024)(128)(4,1)}), s8[4194304]{0:T(1024)(128)(4,1)S(1)}, s32[]{:S(2)}) async-start(s8[16777216]{0:T(1024)(128)(4,1)} %bitcast.152), calls=%async_computation.9 | async-start | bytes 8388608
  721.2 15.7 %slice-start.3 = ((s8[16777216]{0:T(1024)(128)(4,1)}), s8[4194304]{0:T(1024)(128)(4,1)S(1)}, s32[]{:S(2)}) async-start(s8[16777216]{0:T(1024)(128)(4,1)} %bitcast.152), calls=%async_computation.10 | async-start | bytes 8388608
  736.9 26.5 %copy-start.7 = (f32[32,64,128]{2,0,1:T(8,128)S(1)}, f32[32,64,128]{2,0,1:T(8,128)}, u32[]{:S(2)}) copy-start(f32[32,64,128]{2,0,1:T(8,128)} %copy-done.6) | copy-start | bytes 3145732
  830.6 33.3 %copy-start.10 = (f32[16,128]{1,0:T(8,128)S(1)}, f32[16,128]{1,0:T(8,128)}, u32[]{:S(2)}) copy-start(f32[16,128]{1,0:T(8,128)} %param.26) | copy-start | bytes 24580
Sparse Core Ops, SparseCore 0:
  123.0 35.7 all-gather.20
  160.5 32.0 all-gather.14
  195.3 51.1 all-gather.12
  336.7 54.9 all-gather.16
  498.6 54.9 all-gather.22
  717.8 32.1 all-gather.18
  799.0 63.4 all-gather.24
